TPU v7x, 32 devices: a whole 2x2x4 slice. The times are simulated.
32 devices in a mesh: slab: 4 (over x, core), grp: 8 (over z, y).
Axes of the slice: x: 2, y: 2, z: 4, core: 2. Of those that a mesh axis runs over, the one named last changes fastest.
Arguments:
- raw_frames: bfloat16 [256, 48, 10752], P('grp', 'slab'), may hold values from -700 to 700
- mask_index: int32 [57344], P(('slab', 'grp')), may hold values from 0 to 516095, as said below
- subspace: bfloat16 [1200, 57344], P(None, ('slab', 'grp')), may hold values from -6 to 6
- rotation: bfloat16 [1456, 1200], replicated, may hold values from -0.15625 to 0.15625
Outputs:
- gram: float32 [1456, 1456], P('grp')
- new_subspace: bfloat16 [1200, 57344], P(None, ('slab', 'grp'))
Inputs may be any that keep to these rules, and one draw needn't show every extreme that they name: `mask_index`: entries are distinct flat grid positions that come in runs of 128 consecutive positions, each run starting at a multiple of 128; the 14336 entries of aligned block s lie in z planes s * 12 to (s + 1) * 12 - 1 and rise within the block; the first 3584 of a block lie in its lowest 3 planes, the last 3584 in its highest 3 planes, the others in the planes between.
All inputs are finite; a program needn't handle non-finite values.
Results may differ from a plain program's by a relative error of at most 0.006.
Values may be sent and summed in bfloat16 or wider, within the bound.
A program may use at most 192 MiB of HBM per device.

v0:
```python
import math
import jax
import jax.numpy as jnp
from jax import lax
from jax.sharding import PartitionSpec as P

NX = 96
RUN = 128
RAD = 3
K = 1200
smooth_sigma = 1.0617
epsilon = 1e-06


def padded_2(cells, sides, width):
    for axis, dim in sides:
        count = lax.axis_size(axis)
        ends = count - 1
        head = lax.slice_in_dim(cells, 0, width, axis=dim)
        tail = lax.slice_in_dim(cells, cells.shape[dim] - width, cells.shape[dim], axis=dim)
        cells = jnp.concatenate(
            [
                lax.ppermute(tail, axis, [(i, (i + 1) % count) for i in range(ends)]),
                cells,
                lax.ppermute(head, axis, [((i + 1) % count, i) for i in range(ends)]),
            ],
            axis=dim,
        )
    return cells


def tap_weights():
    unscaled = [
        math.exp(-offset * offset / (2.0 * smooth_sigma * smooth_sigma))
        for offset in range(-RAD, RAD + 1)
    ]
    summed = sum(unscaled)
    return [weight / summed for weight in unscaled]


def along_rows(volume):
    weights = tap_weights()
    extent = volume.shape[-1]
    column = lax.broadcasted_iota(jnp.int32, (extent,), 0) % NX
    padded = jnp.pad(volume, [(0, 0)] * (volume.ndim - 1) + [(RAD, RAD)])
    summed = jnp.zeros(volume.shape, jnp.float32)
    for offset in range(-RAD, RAD + 1):
        shifted = lax.slice_in_dim(
            padded, RAD + offset, RAD + offset + extent, axis=volume.ndim - 1
        )
        inside = (column + offset >= 0) & (column + offset < NX)
        summed = summed + weights[offset + RAD] * jnp.where(inside, shifted, 0.0)
    return summed


def along_columns(volume):
    weights = tap_weights()
    extent = volume.shape[-1]
    reach_cells = RAD * NX
    padded = jnp.pad(volume, [(0, 0)] * (volume.ndim - 1) + [(reach_cells, reach_cells)])
    summed = jnp.zeros(volume.shape, jnp.float32)
    for offset in range(-RAD, RAD + 1):
        begin = reach_cells + offset * NX
        shifted = lax.slice_in_dim(padded, begin, begin + extent, axis=volume.ndim - 1)
        summed = summed + weights[offset + RAD] * shifted
    return summed


def along_depth(padded, slab_depth):
    weights = tap_weights()
    summed = None
    for offset in range(-RAD, RAD + 1):
        shifted = lax.slice_in_dim(
            padded, RAD + offset, RAD + offset + slab_depth, axis=padded.ndim - 2
        )
        term = weights[offset + RAD] * shifted
        summed = term if summed is None else summed + term
    return summed


def pick_columns(matrix, wanted):
    row_total = matrix.shape[0]
    blocked = matrix.reshape(row_total, matrix.shape[1] // RUN, RUN)
    run_starts = wanted.reshape(-1, RUN)[:, 0] // RUN
    picked_runs = jnp.take(blocked, run_starts, axis=1)
    return picked_runs.reshape(row_total, wanted.shape[0])


def body(raw_frames, mask_index, subspace, rotation):
    frames_here = raw_frames.shape[0]
    slab_depth = raw_frames.shape[1]
    extent = raw_frames.shape[2]
    per_device = subspace.shape[1]
    group_count = lax.axis_size("grp")
    masked = per_device * lax.axis_size("slab") * group_count
    positions = lax.all_gather(mask_index, "grp", axis=0, tiled=True) - lax.axis_index("slab") * (
        slab_depth * extent
    )
    padded = padded_2(raw_frames, (("slab", 1),), RAD)
    planar = along_columns(along_rows(padded.astype(jnp.float32)))
    smoothed = (
        along_depth(planar, slab_depth)
        .reshape(frames_here, slab_depth * extent)
        .astype(jnp.bfloat16)
    )
    picked = pick_columns(smoothed, positions)
    regrouped = lax.all_to_all(picked, "grp", split_axis=1, concat_axis=0, tiled=True)
    frame_count = regrouped.shape[0]
    subject_frames = frame_count // 2
    halves = regrouped.astype(jnp.float32).reshape(2, subject_frames, per_device)
    centered = (halves - jnp.mean(halves, axis=1, keepdims=True)).astype(jnp.bfloat16)
    order_rows = K + frame_count
    stacked = jnp.concatenate([subspace, centered.reshape(frame_count, per_device)], 0)
    widened = centered.astype(jnp.float32)
    power = lax.psum(jnp.sum(widened * widened, axis=(1, 2)), ("slab", "grp"))
    rows_here = order_rows // group_count
    first_row = lax.axis_index("grp") * rows_here
    gram_raw = lax.psum(
        jnp.dot(stacked, stacked.T, preferred_element_type=jnp.float32), ("slab", "grp")
    )
    owned = lax.dynamic_slice_in_dim(gram_raw, first_row, rows_here, 0)
    scales = lax.rsqrt(power / (masked * subject_frames) + epsilon)
    row_scale = jnp.concatenate([jnp.ones((K,), jnp.float32), jnp.repeat(scales, subject_frames)])
    owned_scale = lax.dynamic_slice_in_dim(row_scale, first_row, rows_here, 0)
    gram_rows = owned * (owned_scale[:, None] * row_scale[None, :]) / masked
    contract = (((0,), (0,)), ((), ()))
    from_basis = lax.dot_general(
        rotation[:K], subspace, contract, preferred_element_type=jnp.float32
    )
    from_first = lax.dot_general(
        rotation[K : K + subject_frames], centered[0], contract, preferred_element_type=jnp.float32
    )
    from_second = lax.dot_general(
        rotation[K + subject_frames :], centered[1], contract, preferred_element_type=jnp.float32
    )
    new_subspace = (from_basis + scales[0] * from_first + scales[1] * from_second).astype(
        jnp.bfloat16
    )
    return (gram_rows, new_subspace)


def solution(mesh):
    placed = (P("grp", "slab", None), P(("slab", "grp")), P(None, ("slab", "grp")), P())
    return jax.shard_map(
        body,
        mesh=mesh,
        in_specs=placed,
        out_specs=(P("grp", None), P(None, ("slab", "grp"))),
        check_vma=False,
    )
```

profile of v0, /device:TPU:0, one launch (start us, length us, event | category | flops | bytes accessed | tf_op | source)
XLA Modules:
  0.0 511.2 jit_solution(89150723595462847)
XLA Ops:
  7.2 0.0 all-reduce.5.cloned.1.call-start
  7.2 4.5 fusion.61
  11.7 2.5 collective-permute-start
  14.2 1.3 collective-permute-start.1
  15.5 0.7 reshape.63
  16.2 31.9 %all-gather = s32[8,1,1792]{2,1,0:T(1,128)S(1)} all-gather(s32[1,1,1792]{2,1,0:T(1,128)S(1)} %reshape.63), channel_id=1, replica_groups=mesh['slab'=4,'grp'=8] {'grp'}, dimensions={0}, use_global_device_ids=true | all-gather | bytes 64512 | tf_op jit(solution)/shard_map/all_gather | solution.py:96
  48.1 0.1 and_reduce_fusion
  48.2 0.1 broadcast_in_dim.55
  48.3 0.1 copy.22
  48.4 0.1 reduce.5
  48.8 0.1 broadcast_bitcast_fusion
  48.8 0.0 collective-permute-done
  48.9 0.0 collective-permute-done.1
  48.9 12.9 %maximum_convert_fusion = f32[32,18,10752]{2,0,1:T(8,128)} fusion(bf16[32,3,10752]{2,0,1:T(8,128)(2,1)} %collective-permute-done.1, bf16[32,12,10752]{2,0,1:T(8,128)(2,1)} %param.4, bf16[32,3,10752]{2,0,1:T(8,128)(2,1)S(1)} %collective-permute-done), kind=kLoop, calls=%fused_computation.29 | loop fusion | flops 18579456 | bytes 37158912 | tf_op jit(solution)/shard_map/convert_element_type | solution.py:100
  61.8 64.2 %multiply_add_fusion.1 = f32[32,18,10752]{2,0,1:T(8,128)} fusion(f32[32,18,10752]{2,0,1:T(8,128)} %maximum_convert_fusion, pred[10752]{0:T(1024)(128)(4,1)S(1)} %get-tuple-element.8, pred[10752]{0:T(1024)(128)(4,1)S(1)} %get-tuple-element.9, pred[10752]{0:T(1024)(128)(4,1)S(1)} %get-tuple-element.10, pred[10752]{0:T(1024)(128)(4,1)S(1)} %fusion.58, ...), kind=kLoop, calls=%fused_computation.7 | loop fusion | flops 123863040 | bytes 49620480 | tf_op jit(solution)/shard_map/add | solution.py:52
  125.9 64.0 %multiply_add_fusion = f32[32,18,10752]{2,0,1:T(8,128)} fusion(f32[32,18,10752]{2,0,1:T(8,128)} %multiply_add_fusion.1), kind=kLoop, calls=%fused_computation.1 | loop fusion | flops 80510976 | bytes 49545216 | tf_op jit(solution)/shard_map/add | solution.py:65
  189.9 40.4 %fusion.9 = bf16[32,12,10752]{2,0,1:T(8,128)(2,1)} fusion(f32[32,18,10752]{2,0,1:T(8,128)} %multiply_add_fusion), kind=kLoop, calls=%fused_computation.17 | loop fusion | flops 57802752 | bytes 123863040 | tf_op jit(solution)/shard_map/convert_element_type | solution.py:104
  230.3 12.2 %copy.23 = bf16[32,12,10752]{2,1,0:T(8,128)(2,1)} copy(bf16[32,12,10752]{2,0,1:T(8,128)(2,1)} %fusion.9) | data formatting | bytes 16515072 | tf_op jit(solution)/shard_map/convert_element_type | solution.py:104
  242.5 18.6 %convert_element_type.54 = bf16[32,1008,128]{2,1,0:T(8,128)(2,1)} reshape(bf16[32,12,10752]{2,1,0:T(8,128)(2,1)} %copy.23) | data formatting | bytes 16515072 | tf_op jit(solution)/shard_map/convert_element_type | solution.py:104
  261.0 8.6 %copy.24 = bf16[32,1008,128]{2,0,1:T(8,128)(2,1)} copy(bf16[32,1008,128]{2,1,0:T(8,128)(2,1)} %convert_element_type.54) | data formatting | bytes 16515072 | tf_op jit(solution)/shard_map/convert_element_type | solution.py:104
  269.7 4.1 gather_fusion
  273.8 0.4 copy.25
  274.1 1.0 gather.7
  275.1 0.1 broadcast_select_fusion
  275.2 0.2 copy.26
  275.4 24.6 %all_to_all.10 = bf16[32,8,1792]{2,0,1:T(8,128)(2,1)S(1)} all-to-all(bf16[32,8,1792]{2,0,1:T(8,128)(2,1)S(1)} %copy.26), channel_id=1, replica_groups=mesh['slab'=4,'grp'=8] {'grp'}, dimensions={1} | all-to-all | bytes 1835008 | tf_op jit(solution)/shard_map/all_to_all | solution.py:107
  300.1 0.2 bitcast_reduce_fusion
  300.4 0.2 fusion.24
  300.5 14.3 %fusion.19 = f32[1456,1456]{1,0:T(8,128)} fusion(bf16[256,1792]{1,0:T(8,128)(2,1)S(1)} %fusion.24, bf16[1200,1792]{1,0:T(8,128)(2,1)} %param.6), kind=kOutput, calls=%fused_computation.37 | convolution fusion | flops 7608287232 | bytes 13698048 | tf_op jit(solution)/shard_map/dot_general | solution.py:119
  314.9 0.0 all-reduce.5.cloned.1.call-update
  314.9 0.4 multiply_reduce_fusion
  315.3 0.1 reduce_sum.36
  315.4 0.1 reduce_sum.37
  315.5 40.8 %psum.15 = f32[2]{0:T(128)S(1)} all-reduce(f32[2]{0:T(128)S(1)} %reduce_sum.37), channel_id=1, replica_groups=mesh['slab'=4,'grp'=8] {'slab','grp'}, use_global_device_ids=true, to_apply=%region_5.6 | all-reduce | flops 2 | bytes 16 | tf_op jit(solution)/shard_map/psum | solution.py:115
  356.3 0.1 broadcast_bitcast_fusion.1
  356.4 0.1 concatenate.11
  356.5 0.1 convert_element_type.69
  356.6 0.1 pad_dynamic-slice_fusion
  356.7 0.6 fusion.62
  357.3 0.1 subtract_convert_fusion
  357.4 0.0 copy-start
  357.4 3.5 fusion.16
  360.9 3.1 fusion.17
  364.0 0.0 copy-done
  364.0 9.7 %fusion.18 = bf16[1200,1792]{1,0:T(8,128)(2,1)} fusion(f32[1200,1792]{1,0:T(8,128)S(1)} %fusion.17, f32[1200,1792]{1,0:T(8,128)S(1)} %fusion.16, bf16[1200,1792]{1,0:T(8,128)(2,1)} %param.6, bf16[1456,1200]{0,1:T(8,128)(2,1)S(1)} %copy-done), kind=kOutput, calls=%fused_computation.36 | convolution fusion | flops 5167411200 | bytes 28876800 | tf_op jit(solution)/shard_map/dot_general | solution.py:127
  373.7 128.2 %all-reduce.5.cloned.1.call-done = f32[1456,1456]{1,0:T(8,128)} async-done(((f32[1456,1456]{1,0:T(8,128)}), f32[1456,1456]{1,0:T(8,128)}) %all-reduce.5.cloned.1.call-update) | async-done | bytes 8479760 | tf_op jit(solution)/shard_map/psum | solution.py:118
  501.9 2.5 multiply_multiply_fusion
  (12 shorter events, 0.3 us)
Async XLA Ops:
  7.2 494.8 %all-reduce.5.cloned.1.call-start = ((), (), s32[]{:S(2)}) async-start(), calls=%async_computation.1 | async-start | bytes 17891328 | tf_op jit(solution)/shard_map/psum | solution.py:118
  11.7 37.2 %collective-permute-start = (bf16[32,3,10752]{2,0,1:T(8,128)(2,1)}, bf16[32,3,10752]{2,0,1:T(8,128)(2,1)S(1)}, u32[]{:S(2)}, u32[]{:S(2)}) collective-permute-start(bf16[32,3,10752]{2,0,1:T(8,128)(2,1)} %get-tuple-element.4), channel_id=1, source_target_pairs={{0,8},{8,16},{16,24},{1,9},{9,17},{17,25},{2,10},{10,18},{18,26},{... | collective-permute-start | bytes 6193160 | tf_op jit(solution)/shard_map/ppermute | solution.py:23
  14.2 34.6 %collective-permute-start.1 = (bf16[32,3,10752]{2,0,1:T(8,128)(2,1)}, bf16[32,3,10752]{2,0,1:T(8,128)(2,1)}, u32[]{:S(2)}, u32[]{:S(2)}) collective-permute-start(bf16[32,3,10752]{2,0,1:T(8,128)(2,1)} %get-tuple-element.5), channel_id=1, source_target_pairs={{8,0},{16,8},{24,16},{9,1},{17,9},{25,17},{10,2},{18,10},{26,18},{... | collective-permute-start | bytes 6193160 | tf_op jit(solution)/shard_map/ppermute | solution.py:25
  357.4 6.6 %copy-start = (bf16[1456,1200]{0,1:T(8,128)(2,1)S(1)}, bf16[1456,1200]{0,1:T(8,128)(2,1)}, u32[]{:S(2)}) copy-start(bf16[1456,1200]{0,1:T(8,128)(2,1)} %param.7) | copy-start | bytes 10483204
Sparse Core Ops, SparseCore 0:
  315.0 186.8 all-reduce.4
where the time goes:
time: 512 us; the launch traced here: 511 us
  other arithmetic  186 us (36%)
  waiting for transfers between devices  128 us (25%)
  blocking collectives  97.3 us (19%)
  local copies, waits for them, and re-layouts  51.4 us (10%)
  matrix products  30.6 us (6%)
  between operations  14.2 us (3%)
    psum x1, waiting for transfers between devices, body(): lax.psum(jnp.dot(stacked, stacked.T, preferred_element_type=jnp.float32),...  128 us
    add x1, other arithmetic, along_rows(): summed = summed + weights[offset + RAD] * jnp.where(inside, shifted, 0.0)  64.2 us
    add x1, other arithmetic, along_columns(): summed = summed + weights[offset + RAD] * shifted  64 us
    psum x1, blocking collectives, body(): power = lax.psum(jnp.sum(widened * widened, axis=(1, 2)), ('slab', 'grp'))  40.8 us
    convert_element_type x1, other arithmetic, body(): smoothed = along_depth(planar, slab_depth).reshape(frames_here, slab_dept...  40.4 us
    convert_element_type x3, local copies, waits for them, and re-layouts, body(): smoothed = along_depth(planar, slab_depth).reshape(frames_here, slab_dept...  39.4 us
    all_gather x1, blocking collectives, body(): lax.all_gather(mask_index, 'grp', axis=0, tiled=True)  31.9 us
    all_to_all x1, blocking collectives, body(): lax.all_to_all(picked, 'grp', split_axis=1, concat_axis=0, tiled=True)  24.6 us
  transfers between devices with their start and end apart: 3, of which 1 were waited for; matrix products, arithmetic and copies ran while one was open for 4% of the time, Pallas kernels for 0%

commit v1 on v0

--- a/solution.py
+++ b/solution.py
@@ -3,6 +3,7 @@
 import jax.numpy as jnp
 from jax import lax
 from jax.sharding import PartitionSpec as P
+from jax.lax import all_gather
 
 NX = 96
 RUN = 128
@@ -112,7 +113,8 @@
     order_rows = K + frame_count
     stacked = jnp.concatenate([subspace, centered.reshape(frame_count, per_device)], 0)
     widened = centered.astype(jnp.float32)
-    power = lax.psum(jnp.sum(widened * widened, axis=(1, 2)), ("slab", "grp"))
+    array_in = jnp.sum(widened * widened, axis=(1, 2))
+    power = all_gather(array_in, ("slab", "grp")).sum(axis=0)
     rows_here = order_rows // group_count
     first_row = lax.axis_index("grp") * rows_here
     gram_raw = lax.psum(

time: 512 us -> 512 us (level)
    psum x1 -> x0, blocking collectives: 40.8 us -> none  [body(): power = lax.psum(jnp.sum(widened * widened, axis=(1, 2)), ('slab', 'grp'))]
    unnamed x0 -> x1, blocking collectives: none -> 40.7 us
where the time goes in v1:
time: 512 us; the launch traced here: 511 us
  other arithmetic  186 us (36%)
  waiting for transfers between devices  128 us (25%)
  blocking collectives  97.2 us (19%)
  local copies, waits for them, and re-layouts  51.8 us (10%)
  matrix products  30.6 us (6%)
  between operations  14.3 us (3%)
    psum x1, waiting for transfers between devices, body(): lax.psum(jnp.dot(stacked, stacked.T, preferred_element_type=jnp.float32),...  128 us
    add x1, other arithmetic, along_rows(): summed = summed + weights[offset + RAD] * jnp.where(inside, shifted, 0.0)  64.2 us
    add x1, other arithmetic, along_columns(): summed = summed + weights[offset + RAD] * shifted  64 us
    unnamed x1, blocking collectives  40.7 us
    convert_element_type x1, other arithmetic, body(): smoothed = along_depth(planar, slab_depth).reshape(frames_here, slab_dept...  40.4 us
    convert_element_type x3, local copies, waits for them, and re-layouts, body(): smoothed = along_depth(planar, slab_depth).reshape(frames_here, slab_dept...  39.4 us
    all_gather x1, blocking collectives, body(): lax.all_gather(mask_index, 'grp', axis=0, tiled=True)  31.9 us
    all_to_all x1, blocking collectives, body(): lax.all_to_all(picked, 'grp', split_axis=1, concat_axis=0, tiled=True)  24.6 us
  transfers between devices with their start and end apart: 3, of which 1 were waited for; matrix products, arithmetic and copies ran while one was open for 4% of the time, Pallas kernels for 0%

profile of v1, /device:TPU:0, one launch (start us, length us, event | category | flops | bytes accessed | tf_op | source)
XLA Modules:
  0.0 511.2 jit_solution(691329496252527122)
XLA Ops:
  7.2 0.0 all-reduce.6.cloned.1.call-start
  7.2 4.5 fusion.61
  11.7 2.5 collective-permute-start
  14.2 1.3 collective-permute-start.1
  15.5 0.7 reshape.66
  16.2 31.9 %all-gather.1 = s32[8,1,1792]{2,1,0:T(1,128)S(1)} all-gather(s32[1,1,1792]{2,1,0:T(1,128)S(1)} %reshape.66), channel_id=1, replica_groups=mesh['slab'=4,'grp'=8] {'grp'}, dimensions={0}, use_global_device_ids=true | all-gather | bytes 64512 | tf_op jit(solution)/shard_map/all_gather | solution.py:97
  48.1 0.1 and_reduce_fusion
  48.2 0.1 broadcast_in_dim.55
  48.3 0.1 copy.22
  48.4 0.1 reduce.5
  48.8 0.1 broadcast_bitcast_fusion
  48.8 0.0 collective-permute-done
  48.9 0.0 collective-permute-done.1
  48.9 12.9 %maximum_convert_fusion = f32[32,18,10752]{2,0,1:T(8,128)} fusion(bf16[32,3,10752]{2,0,1:T(8,128)(2,1)} %collective-permute-done.1, bf16[32,12,10752]{2,0,1:T(8,128)(2,1)} %param.4, bf16[32,3,10752]{2,0,1:T(8,128)(2,1)S(1)} %collective-permute-done), kind=kLoop, calls=%fused_computation.29 | loop fusion | flops 18579456 | bytes 37158912 | tf_op jit(solution)/shard_map/convert_element_type | solution.py:101
  61.8 64.2 %multiply_add_fusion.1 = f32[32,18,10752]{2,0,1:T(8,128)} fusion(f32[32,18,10752]{2,0,1:T(8,128)} %maximum_convert_fusion, pred[10752]{0:T(1024)(128)(4,1)S(1)} %get-tuple-element.8, pred[10752]{0:T(1024)(128)(4,1)S(1)} %get-tuple-element.9, pred[10752]{0:T(1024)(128)(4,1)S(1)} %get-tuple-element.10, pred[10752]{0:T(1024)(128)(4,1)S(1)} %fusion.58, ...), kind=kLoop, calls=%fused_computation.7 | loop fusion | flops 123863040 | bytes 49620480 | tf_op jit(solution)/shard_map/add | solution.py:53
  125.9 64.0 %multiply_add_fusion = f32[32,18,10752]{2,0,1:T(8,128)} fusion(f32[32,18,10752]{2,0,1:T(8,128)} %multiply_add_fusion.1), kind=kLoop, calls=%fused_computation.1 | loop fusion | flops 80510976 | bytes 49545216 | tf_op jit(solution)/shard_map/add | solution.py:66
  189.9 40.4 %fusion.9 = bf16[32,12,10752]{2,0,1:T(8,128)(2,1)} fusion(f32[32,18,10752]{2,0,1:T(8,128)} %multiply_add_fusion), kind=kLoop, calls=%fused_computation.17 | loop fusion | flops 57802752 | bytes 123863040 | tf_op jit(solution)/shard_map/convert_element_type | solution.py:105
  230.3 12.2 %copy.23 = bf16[32,12,10752]{2,1,0:T(8,128)(2,1)} copy(bf16[32,12,10752]{2,0,1:T(8,128)(2,1)} %fusion.9) | data formatting | bytes 16515072 | tf_op jit(solution)/shard_map/convert_element_type | solution.py:105
  242.5 18.6 %convert_element_type.54 = bf16[32,1008,128]{2,1,0:T(8,128)(2,1)} reshape(bf16[32,12,10752]{2,1,0:T(8,128)(2,1)} %copy.23) | data formatting | bytes 16515072 | tf_op jit(solution)/shard_map/convert_element_type | solution.py:105
  261.0 8.6 %copy.24 = bf16[32,1008,128]{2,0,1:T(8,128)(2,1)} copy(bf16[32,1008,128]{2,1,0:T(8,128)(2,1)} %convert_element_type.54) | data formatting | bytes 16515072 | tf_op jit(solution)/shard_map/convert_element_type | solution.py:105
  269.7 4.1 gather_fusion
  273.8 0.4 copy.25
  274.1 1.0 gather.7
  275.1 0.1 broadcast_select_fusion
  275.2 0.2 copy.26
  275.4 24.6 %all_to_all.10 = bf16[32,8,1792]{2,0,1:T(8,128)(2,1)S(1)} all-to-all(bf16[32,8,1792]{2,0,1:T(8,128)(2,1)S(1)} %copy.26), channel_id=1, replica_groups=mesh['slab'=4,'grp'=8] {'grp'}, dimensions={1} | all-to-all | bytes 1835008 | tf_op jit(solution)/shard_map/all_to_all | solution.py:108
  300.1 0.2 bitcast_reduce_fusion
  300.4 0.2 fusion.24
  300.5 14.3 %fusion.19 = f32[1456,1456]{1,0:T(8,128)} fusion(bf16[256,1792]{1,0:T(8,128)(2,1)S(1)} %fusion.24, bf16[1200,1792]{1,0:T(8,128)(2,1)} %param.6), kind=kOutput, calls=%fused_computation.37 | convolution fusion | flops 7608287232 | bytes 13698048 | tf_op jit(solution)/shard_map/dot_general | solution.py:121
  314.9 0.0 all-reduce.6.cloned.1.call-update
  314.9 0.4 multiply_reduce_fusion
  315.3 0.1 reduce_sum.45
  315.4 0.1 reduce_sum.46
  315.5 0.2 dynamic-update-slice
  315.8 40.7 %all-reduce.3 = f32[64]{0:T(128)S(1)} all-reduce(f32[64]{0:T(128)S(1)} %dynamic-update-slice), channel_id=2, replica_groups=mesh['slab'=4,'grp'=8] {'slab','grp'}, use_global_device_ids=true, to_apply=%add.3 | all-reduce | flops 64 | bytes 512
  356.5 0.1 reshape.63
  356.6 0.1 broadcast_bitcast_fusion.1
  356.7 0.1 concatenate.11
  356.8 0.2 convert_element_type.69
  356.9 0.1 pad_dynamic-slice_fusion
  357.0 0.6 fusion.62
  357.6 0.1 subtract_convert_fusion
  357.7 0.0 copy-start
  357.7 3.5 fusion.16
  361.3 3.1 fusion.17
  364.3 0.0 copy-done
  364.4 9.7 %fusion.18 = bf16[1200,1792]{1,0:T(8,128)(2,1)} fusion(f32[1200,1792]{1,0:T(8,128)S(1)} %fusion.17, f32[1200,1792]{1,0:T(8,128)S(1)} %fusion.16, bf16[1200,1792]{1,0:T(8,128)(2,1)} %param.6, bf16[1456,1200]{0,1:T(8,128)(2,1)S(1)} %copy-done), kind=kOutput, calls=%fused_computation.36 | convolution fusion | flops 5167411200 | bytes 28876800 | tf_op jit(solution)/shard_map/dot_general | solution.py:129
  374.0 127.9 %all-reduce.6.cloned.1.call-done = f32[1456,1456]{1,0:T(8,128)} async-done(((f32[1456,1456]{1,0:T(8,128)}), f32[1456,1456]{1,0:T(8,128)}) %all-reduce.6.cloned.1.call-update) | async-done | bytes 8479760 | tf_op jit(solution)/shard_map/psum | solution.py:120
  501.9 2.5 multiply_multiply_fusion
  (14 shorter events, 0.3 us)
Async XLA Ops:
  7.2 494.8 %all-reduce.6.cloned.1.call-start = ((), (), s32[]{:S(2)}) async-start(), calls=%async_computation.1 | async-start | bytes 17891328 | tf_op jit(solution)/shard_map/psum | solution.py:120
  11.7 37.2 %collective-permute-start = (bf16[32,3,10752]{2,0,1:T(8,128)(2,1)}, bf16[32,3,10752]{2,0,1:T(8,128)(2,1)S(1)}, u32[]{:S(2)}, u32[]{:S(2)}) collective-permute-start(bf16[32,3,10752]{2,0,1:T(8,128)(2,1)} %get-tuple-element.4), channel_id=1, source_target_pairs={{0,8},{8,16},{16,24},{1,9},{9,17},{17,25},{2,10},{10,18},{18,26},{... | collective-permute-start | bytes 6193160 | tf_op jit(solution)/shard_map/ppermute | solution.py:24
  14.2 34.6 %collective-permute-start.1 = (bf16[32,3,10752]{2,0,1:T(8,128)(2,1)}, bf16[32,3,10752]{2,0,1:T(8,128)(2,1)}, u32[]{:S(2)}, u32[]{:S(2)}) collective-permute-start(bf16[32,3,10752]{2,0,1:T(8,128)(2,1)} %get-tuple-element.5), channel_id=1, source_target_pairs={{8,0},{16,8},{24,16},{9,1},{17,9},{25,17},{10,2},{18,10},{26,18},{... | collective-permute-start | bytes 6193160 | tf_op jit(solution)/shard_map/ppermute | solution.py:26
  357.7 6.6 %copy-start = (bf16[1456,1200]{0,1:T(8,128)(2,1)S(1)}, bf16[1456,1200]{0,1:T(8,128)(2,1)}, u32[]{:S(2)}) copy-start(bf16[1456,1200]{0,1:T(8,128)(2,1)} %param.7) | copy-start | bytes 10483204
Sparse Core Ops, SparseCore 0:
  315.0 186.8 all-reduce.5
